TPU v7x, 256 devices: a whole 4x4x8 slice. The times are simulated.
256 devices in a mesh: row: 8 (over x, core), col: 32 (over y, z).
Axes of the slice: x: 4, y: 4, z: 8, core: 2. Of those that a mesh axis runs over, the one named last changes fastest.
Arguments:
- upper_panel: float32 [2048, 8192], P('row', 'col')
- lower_panel: float32 [2048, 8192], P('row', 'col')
- pole_values: float32 [2, 8192], P(None, 'col'), may hold values from 0 to 4, as said below
- coupling: float32 [2, 8192], P(None, 'col'), may hold values from -6 to 6
- kept_mask: int32 [2, 8192], P(None, 'col'), may hold values from 0 to 1, as said below
- shifts: float32 [16384], P('col'), may hold values from 0 to 4
- source: int32 [16384], P('col'), may hold values from 0 to 16384, as said below
Outputs:
- vectors: float32 [2, 2048, 16384], P(None, 'row', 'col')
- slab_weight: float32 [16384], P('col')
Inputs may be any that keep to these rules, and one draw needn't show every extreme that they name: source[j] = 16384 marks an undeflated merged column; any other value is the pole whose child column the merged column copies, and no pole is named twice. Each device's 512 merged columns hold from 64 to 384 undeflated columns, and some device holds exactly 384. kept_mask is 0 exactly at the poles named in source. Some device of col holds no deflated pole: every pole of both children that it holds is kept. `pole_values`: every pole lies at least 0.4 / 16384 away from every entry of shifts.
All inputs are finite; a program needn't handle non-finite values.
Results may differ from a plain program's by a relative error of at most 0.0003.
Values sent between devices are 32-bit elements; how exact they have to be, the bound alone decides.
A program may use at most 64 MiB of HBM per device.

v0:
```python
import math
import jax
import jax.numpy as jnp
from jax import lax
from jax.sharding import PartitionSpec as P

N1 = 8192
exact_mode = lax.Precision.HIGHEST


def cauchy_block(pole_vals, weights, shift_vals):
    return weights[:, :, None] / (pole_vals[:, :, None] - shift_vals[None, None, :])


def local(upper_panel, lower_panel, pole_values, coupling, kept_mask, shifts, source):
    rows_here = upper_panel.shape[0]
    own_cols = shifts.shape[0]
    weighted = coupling * kept_mask.astype(jnp.float32)
    undeflated = source == 2 * N1
    child_base = jnp.array([0, N1], jnp.int32)
    zeros_acc = jnp.zeros((rows_here, own_cols), jnp.float32)
    pieces = (
        lax.all_gather(upper_panel, "col", axis=1, tiled=True),
        lax.all_gather(lower_panel, "col", axis=1, tiled=True),
        lax.all_gather(pole_values, "col", axis=1, tiled=True),
        lax.all_gather(weighted, "col", axis=1, tiled=True),
    )
    span_cols = math.gcd(pieces[0].shape[1], 1024)

    def advance(number, running):
        window = [
            lax.dynamic_slice_in_dim(member, number * span_cols, span_cols, 1) for member in pieces
        ]
        first_pole = number * span_cols
        cauchy = cauchy_block(window[2], window[3], shifts)
        indices = first_pole + lax.iota(jnp.int32, span_cols)
        one_hot = indices[None, :, None] + child_base[:, None, None] == source[None, None, :]
        basis_tile = jnp.where(undeflated[None, None, :], cauchy, one_hot.astype(jnp.float32))
        upper_acc = running[0] + jnp.dot(
            window[0], basis_tile[0], precision=exact_mode, preferred_element_type=jnp.float32
        )
        lower_acc = running[1] + jnp.dot(
            window[1], basis_tile[1], precision=exact_mode, preferred_element_type=jnp.float32
        )
        return (upper_acc, lower_acc, running[2] + jnp.sum(cauchy * cauchy, axis=(0, 1)))

    upper_acc, lower_acc, norm_sums = lax.fori_loop(
        0,
        pieces[0].shape[1] // span_cols,
        advance,
        (zeros_acc, zeros_acc, jnp.zeros((own_cols,), jnp.float32)),
    )
    scaling = jnp.where(undeflated, lax.rsqrt(norm_sums), 1.0)
    vectors = jnp.stack([upper_acc * scaling[None, :], lower_acc * scaling[None, :]])
    partial_weight = jnp.sum(vectors * vectors, axis=(0, 1))
    slab_weight = lax.psum(partial_weight, "row") / (2 * rows_here * lax.axis_size("row"))
    return (vectors, slab_weight)


def solution(mesh):
    in_specs = (
        P("row", "col"),
        P("row", "col"),
        P(None, "col"),
        P(None, "col"),
        P(None, "col"),
        P("col"),
        P("col"),
    )
    out_specs = (P(None, "row", "col"), P("col"))
    return jax.shard_map(local, mesh=mesh, in_specs=in_specs, out_specs=out_specs, check_vma=False)
```

profile of v0, /device:TPU:1, one launch (start us, length us, event | category | flops | bytes accessed | tf_op | source)
XLA Modules:
  0.0 310.2 jit_solution(16482954497444541827)
XLA Ops:
  8.7 0.7 convert_multiply_fusion
  9.4 41.5 %all_gather.13 = f32[2,8192]{1,0:T(2,128)S(1)} all-gather(f32[2,256]{1,0:T(2,128)S(1)} %convert_multiply_fusion), channel_id=1, replica_groups=mesh['row'=8,'col'=32] {'col'}, dimensions={1}, use_global_device_ids=true | all-gather | bytes 67584 | tf_op jit(solution)/shard_map/all_gather | solution.py:26
  50.9 39.2 %all_gather.14 = f32[2,8192]{1,0:T(2,128)S(1)} all-gather(f32[2,256]{1,0:T(2,128)} %param.12), channel_id=1, replica_groups=mesh['row'=8,'col'=32] {'col'}, dimensions={1}, use_global_device_ids=true | all-gather | bytes 67584 | tf_op jit(solution)/shard_map/all_gather | solution.py:25
  90.8 23.1 %all-gather.3.cloned.1.call-done = f32[256,8192]{1,0:T(8,128)} async-done(((f32[256,256]{1,0:T(8,128)}), f32[256,8192]{1,0:T(8,128)}) %all-gather.3.cloned.1.call-update) | async-done | bytes 8388624 | tf_op jit(solution)/shard_map/all_gather | solution.py:23
  113.9 102.9 %all-gather.5.cloned.1.call-done = f32[256,8192]{1,0:T(8,128)} async-done(((f32[256,256]{1,0:T(8,128)}), f32[256,8192]{1,0:T(8,128)}) %all-gather.5.cloned.1.call-update) | async-done | bytes 8388624 | tf_op jit(solution)/shard_map/all_gather | solution.py:24
  216.8 68.3 %while.18 = (s32[]{:T(128)}, f32[256,512]{1,0:T(8,128)S(1)}, f32[256,512]{1,0:T(8,128)S(1)}, f32[512]{0:T(512)S(1)}, f32[256,8192]{1,0:T(8,128)}, /*index=5*/pre...) while((s32[]{:T(128)}, f32[256,512]{1,0:T(8,128)S(1)}, ...), condition=%wide.region_2.3_spmd.clone, body=%wide.region_0.2_spmd.clone.sunk | while | flops 3229093376 | bytes 12669679 | solution.py:47
  216.9 1.9 multiply_reduce_fusion.3
  218.8 3.3 %fusion.17 = f32[256,512]{1,0:T(8,128)S(1)} fusion(f32[2,1024,512]{2,1,0:T(8,128)S(1)} %get-tuple-element.347, f32[256,8192]{1,0:T(8,128)} %get-tuple-element.389, s32[]{:T(128)S(6)} %select_n.28, f32[256,512]{1,0:T(8,128)S(1)} %get-tuple-element.366, pred[]{:T(512)S(6)} %compare.3), kind=kOutput, calls=%fused_computation.9.clone.1 | convolution fusion | flops 1610874880 | bytes 4194309 | tf_op jit(solution)/shard_map/while/body/eval_jaxpr/dot_general | solution.py:42
  222.1 3.3 %fusion.16 = f32[256,512]{1,0:T(8,128)S(1)} fusion(f32[2,1024,512]{2,1,0:T(8,128)S(1)} %get-tuple-element.347, f32[256,8192]{1,0:T(8,128)} %get-tuple-element.383, s32[]{:T(128)S(6)} %select_n.28, f32[256,512]{1,0:T(8,128)S(1)} %get-tuple-element.365, pred[]{:T(512)S(6)} %compare.3), kind=kOutput, calls=%fused_computation.8.clone.1 | convolution fusion | flops 1610874880 | bytes 4194309 | tf_op jit(solution)/shard_map/while/body/eval_jaxpr/dot_general | solution.py:39
  225.5 1.9 multiply_reduce_fusion.3
  227.4 3.3 %fusion.17 = f32[256,512]{1,0:T(8,128)S(1)} fusion(f32[2,1024,512]{2,1,0:T(8,128)S(1)} %get-tuple-element.347, f32[256,8192]{1,0:T(8,128)} %get-tuple-element.389, s32[]{:T(128)S(6)} %select_n.28, f32[256,512]{1,0:T(8,128)S(1)} %get-tuple-element.366, pred[]{:T(512)S(6)} %compare.3), kind=kOutput, calls=%fused_computation.9.clone.1 | convolution fusion | flops 1610874880 | bytes 4194309 | tf_op jit(solution)/shard_map/while/body/eval_jaxpr/dot_general | solution.py:42
  230.6 3.3 %fusion.16 = f32[256,512]{1,0:T(8,128)S(1)} fusion(f32[2,1024,512]{2,1,0:T(8,128)S(1)} %get-tuple-element.347, f32[256,8192]{1,0:T(8,128)} %get-tuple-element.383, s32[]{:T(128)S(6)} %select_n.28, f32[256,512]{1,0:T(8,128)S(1)} %get-tuple-element.365, pred[]{:T(512)S(6)} %compare.3), kind=kOutput, calls=%fused_computation.8.clone.1 | convolution fusion | flops 1610874880 | bytes 4194309 | tf_op jit(solution)/shard_map/while/body/eval_jaxpr/dot_general | solution.py:39
  234.0 1.9 multiply_reduce_fusion.3
  235.9 3.3 %fusion.17 = f32[256,512]{1,0:T(8,128)S(1)} fusion(f32[2,1024,512]{2,1,0:T(8,128)S(1)} %get-tuple-element.347, f32[256,8192]{1,0:T(8,128)} %get-tuple-element.389, s32[]{:T(128)S(6)} %select_n.28, f32[256,512]{1,0:T(8,128)S(1)} %get-tuple-element.366, pred[]{:T(512)S(6)} %compare.3), kind=kOutput, calls=%fused_computation.9.clone.1 | convolution fusion | flops 1610874880 | bytes 4194309 | tf_op jit(solution)/shard_map/while/body/eval_jaxpr/dot_general | solution.py:42
  239.2 3.3 %fusion.16 = f32[256,512]{1,0:T(8,128)S(1)} fusion(f32[2,1024,512]{2,1,0:T(8,128)S(1)} %get-tuple-element.347, f32[256,8192]{1,0:T(8,128)} %get-tuple-element.383, s32[]{:T(128)S(6)} %select_n.28, f32[256,512]{1,0:T(8,128)S(1)} %get-tuple-element.365, pred[]{:T(512)S(6)} %compare.3), kind=kOutput, calls=%fused_computation.8.clone.1 | convolution fusion | flops 1610874880 | bytes 4194309 | tf_op jit(solution)/shard_map/while/body/eval_jaxpr/dot_general | solution.py:39
  242.6 1.9 multiply_reduce_fusion.3
  244.5 3.3 %fusion.17 = f32[256,512]{1,0:T(8,128)S(1)} fusion(f32[2,1024,512]{2,1,0:T(8,128)S(1)} %get-tuple-element.347, f32[256,8192]{1,0:T(8,128)} %get-tuple-element.389, s32[]{:T(128)S(6)} %select_n.28, f32[256,512]{1,0:T(8,128)S(1)} %get-tuple-element.366, pred[]{:T(512)S(6)} %compare.3), kind=kOutput, calls=%fused_computation.9.clone.1 | convolution fusion | flops 1610874880 | bytes 4194309 | tf_op jit(solution)/shard_map/while/body/eval_jaxpr/dot_general | solution.py:42
  247.7 3.3 %fusion.16 = f32[256,512]{1,0:T(8,128)S(1)} fusion(f32[2,1024,512]{2,1,0:T(8,128)S(1)} %get-tuple-element.347, f32[256,8192]{1,0:T(8,128)} %get-tuple-element.383, s32[]{:T(128)S(6)} %select_n.28, f32[256,512]{1,0:T(8,128)S(1)} %get-tuple-element.365, pred[]{:T(512)S(6)} %compare.3), kind=kOutput, calls=%fused_computation.8.clone.1 | convolution fusion | flops 1610874880 | bytes 4194309 | tf_op jit(solution)/shard_map/while/body/eval_jaxpr/dot_general | solution.py:39
  251.1 1.9 multiply_reduce_fusion.3
  253.0 3.3 %fusion.17 = f32[256,512]{1,0:T(8,128)S(1)} fusion(f32[2,1024,512]{2,1,0:T(8,128)S(1)} %get-tuple-element.347, f32[256,8192]{1,0:T(8,128)} %get-tuple-element.389, s32[]{:T(128)S(6)} %select_n.28, f32[256,512]{1,0:T(8,128)S(1)} %get-tuple-element.366, pred[]{:T(512)S(6)} %compare.3), kind=kOutput, calls=%fused_computation.9.clone.1 | convolution fusion | flops 1610874880 | bytes 4194309 | tf_op jit(solution)/shard_map/while/body/eval_jaxpr/dot_general | solution.py:42
  256.3 3.3 %fusion.16 = f32[256,512]{1,0:T(8,128)S(1)} fusion(f32[2,1024,512]{2,1,0:T(8,128)S(1)} %get-tuple-element.347, f32[256,8192]{1,0:T(8,128)} %get-tuple-element.383, s32[]{:T(128)S(6)} %select_n.28, f32[256,512]{1,0:T(8,128)S(1)} %get-tuple-element.365, pred[]{:T(512)S(6)} %compare.3), kind=kOutput, calls=%fused_computation.8.clone.1 | convolution fusion | flops 1610874880 | bytes 4194309 | tf_op jit(solution)/shard_map/while/body/eval_jaxpr/dot_general | solution.py:39
  259.6 1.9 multiply_reduce_fusion.3
  261.5 3.3 %fusion.17 = f32[256,512]{1,0:T(8,128)S(1)} fusion(f32[2,1024,512]{2,1,0:T(8,128)S(1)} %get-tuple-element.347, f32[256,8192]{1,0:T(8,128)} %get-tuple-element.389, s32[]{:T(128)S(6)} %select_n.28, f32[256,512]{1,0:T(8,128)S(1)} %get-tuple-element.366, pred[]{:T(512)S(6)} %compare.3), kind=kOutput, calls=%fused_computation.9.clone.1 | convolution fusion | flops 1610874880 | bytes 4194309 | tf_op jit(solution)/shard_map/while/body/eval_jaxpr/dot_general | solution.py:42
  264.8 3.3 %fusion.16 = f32[256,512]{1,0:T(8,128)S(1)} fusion(f32[2,1024,512]{2,1,0:T(8,128)S(1)} %get-tuple-element.347, f32[256,8192]{1,0:T(8,128)} %get-tuple-element.383, s32[]{:T(128)S(6)} %select_n.28, f32[256,512]{1,0:T(8,128)S(1)} %get-tuple-element.365, pred[]{:T(512)S(6)} %compare.3), kind=kOutput, calls=%fused_computation.8.clone.1 | convolution fusion | flops 1610874880 | bytes 4194309 | tf_op jit(solution)/shard_map/while/body/eval_jaxpr/dot_general | solution.py:39
  268.2 1.9 multiply_reduce_fusion.3
  270.1 3.3 %fusion.17 = f32[256,512]{1,0:T(8,128)S(1)} fusion(f32[2,1024,512]{2,1,0:T(8,128)S(1)} %get-tuple-element.347, f32[256,8192]{1,0:T(8,128)} %get-tuple-element.389, s32[]{:T(128)S(6)} %select_n.28, f32[256,512]{1,0:T(8,128)S(1)} %get-tuple-element.366, pred[]{:T(512)S(6)} %compare.3), kind=kOutput, calls=%fused_computation.9.clone.1 | convolution fusion | flops 1610874880 | bytes 4194309 | tf_op jit(solution)/shard_map/while/body/eval_jaxpr/dot_general | solution.py:42
  273.3 3.3 %fusion.16 = f32[256,512]{1,0:T(8,128)S(1)} fusion(f32[2,1024,512]{2,1,0:T(8,128)S(1)} %get-tuple-element.347, f32[256,8192]{1,0:T(8,128)} %get-tuple-element.383, s32[]{:T(128)S(6)} %select_n.28, f32[256,512]{1,0:T(8,128)S(1)} %get-tuple-element.365, pred[]{:T(512)S(6)} %compare.3), kind=kOutput, calls=%fused_computation.8.clone.1 | convolution fusion | flops 1610874880 | bytes 4194309 | tf_op jit(solution)/shard_map/while/body/eval_jaxpr/dot_general | solution.py:39
  276.7 1.9 multiply_reduce_fusion.3
  278.6 3.3 %fusion.17 = f32[256,512]{1,0:T(8,128)S(1)} fusion(f32[2,1024,512]{2,1,0:T(8,128)S(1)} %get-tuple-element.347, f32[256,8192]{1,0:T(8,128)} %get-tuple-element.389, s32[]{:T(128)S(6)} %select_n.28, f32[256,512]{1,0:T(8,128)S(1)} %get-tuple-element.366, pred[]{:T(512)S(6)} %compare.3), kind=kOutput, calls=%fused_computation.9.clone.1 | convolution fusion | flops 1610874880 | bytes 4194309 | tf_op jit(solution)/shard_map/while/body/eval_jaxpr/dot_general | solution.py:42
  281.9 3.3 %fusion.16 = f32[256,512]{1,0:T(8,128)S(1)} fusion(f32[2,1024,512]{2,1,0:T(8,128)S(1)} %get-tuple-element.347, f32[256,8192]{1,0:T(8,128)} %get-tuple-element.383, s32[]{:T(128)S(6)} %select_n.28, f32[256,512]{1,0:T(8,128)S(1)} %get-tuple-element.365, pred[]{:T(512)S(6)} %compare.3), kind=kOutput, calls=%fused_computation.8.clone.1 | convolution fusion | flops 1610874880 | bytes 4194309 | tf_op jit(solution)/shard_map/while/body/eval_jaxpr/dot_general | solution.py:39
  286.0 1.1 multiply_reduce_fusion.1
  287.1 15.6 %psum.7 = f32[512]{0:T(512)S(1)} all-reduce(f32[512]{0:T(512)S(1)} %get-tuple-element.266), channel_id=1, replica_groups=mesh['row'=8,'col'=32] {'row'}, use_global_device_ids=true, to_apply=%region_4.5 | all-reduce | flops 512 | bytes 4096 | tf_op jit(solution)/shard_map/psum | solution.py:56
  (51 shorter events, 4.3 us)
Async XLA Ops:
  7.2 106.8 %all-gather.3.cloned.1.call-start = ((), (), s32[]{:S(2)}) async-start(), calls=%async_computation | async-start | bytes 8650752 | tf_op jit(solution)/shard_map/all_gather | solution.py:23
  7.9 209.0 %all-gather.5.cloned.1.call-start = ((), (), s32[]{:S(2)}) async-start(), calls=%async_computation.1 | async-start | bytes 8650752 | tf_op jit(solution)/shard_map/all_gather | solution.py:24
Sparse Core Ops, SparseCore 0:
  10.4 103.4 all-gather.2
  116.4 100.4 all-gather.4
where the time goes:
time: 311 us; the launch traced here: 310 us
  waiting for transfers between devices  127 us (41%)
  blocking collectives  96.3 us (31%)
  matrix products  52.1 us (17%)
  other arithmetic  19.7 us (6%)
  between operations  14.1 us (5%)
    all_gather x1, waiting for transfers between devices, local(): lax.all_gather(lower_panel, 'col', axis=1, tiled=True)  103 us
    all_gather x1, blocking collectives, local(): lax.all_gather(weighted, 'col', axis=1, tiled=True)  41.5 us
    all_gather x1, blocking collectives, local(): lax.all_gather(pole_values, 'col', axis=1, tiled=True)  39.2 us
    dot_general x8, matrix products, advance(): jnp.dot(window[0], basis_tile[0], precision=exact_mode, preferred_element...  26 us
    dot_general x8, matrix products, advance(): jnp.dot(window[1], basis_tile[1], precision=exact_mode, preferred_element...  26 us
    all_gather x1, waiting for transfers between devices, local(): lax.all_gather(upper_panel, 'col', axis=1, tiled=True)  23.1 us
    psum x1, blocking collectives, local(): lax.psum(partial_weight, 'row') / (2 * rows_here * lax.axis_size('row'))  15.6 us
    reduce_sum x8, other arithmetic, advance(): jnp.sum(cauchy * cauchy, axis=(0, 1))  15 us
  transfers between devices with their start and end apart: 2, of which 2 were waited for; matrix products, arithmetic and copies ran while one was open for 0% of the time, Pallas kernels for 0%

commit v1 on v0

--- a/solution.py
+++ b/solution.py
@@ -22,7 +22,7 @@
     pieces = (
         lax.all_gather(upper_panel, "col", axis=1, tiled=True),
         lax.all_gather(lower_panel, "col", axis=1, tiled=True),
-        lax.all_gather(pole_values, "col", axis=1, tiled=True),
+        jnp.concatenate(lax.all_gather(pole_values, "col"), axis=1),
         lax.all_gather(weighted, "col", axis=1, tiled=True),
     )
     span_cols = math.gcd(pieces[0].shape[1], 1024)

time: 311 us -> 311 us (level)
  no operation moved by 1% of the time
where the time goes in v1:
time: 311 us; the launch traced here: 310 us
  waiting for transfers between devices  127 us (41%)
  blocking collectives  96.3 us (31%)
  matrix products  52.1 us (17%)
  other arithmetic  19.7 us (6%)
  between operations  14.1 us (5%)
    all_gather x1, waiting for transfers between devices, local(): lax.all_gather(lower_panel, 'col', axis=1, tiled=True)  103 us
    all_gather x1, blocking collectives, local(): lax.all_gather(weighted, 'col', axis=1, tiled=True)  41.5 us
    all_gather x1, blocking collectives, local(): lax.all_gather(pole_values, 'col')  39.2 us
    dot_general x8, matrix products, advance(): jnp.dot(window[0], basis_tile[0], precision=exact_mode, preferred_element...  26 us
    dot_general x8, matrix products, advance(): jnp.dot(window[1], basis_tile[1], precision=exact_mode, preferred_element...  26 us
    all_gather x1, waiting for transfers between devices, local(): lax.all_gather(upper_panel, 'col', axis=1, tiled=True)  23.1 us
    psum x1, blocking collectives, local(): lax.psum(partial_weight, 'row') / (2 * rows_here * lax.axis_size('row'))  15.6 us
    reduce_sum x8, other arithmetic, advance(): jnp.sum(cauchy * cauchy, axis=(0, 1))  15 us
  transfers between devices with their start and end apart: 2, of which 2 were waited for; matrix products, arithmetic and copies ran while one was open for 0% of the time, Pallas kernels for 0%

profile of v1, /device:TPU:1, one launch (start us, length us, event | category | flops | bytes accessed | tf_op | source)
XLA Modules:
  0.0 310.2 jit_solution(5609160749761621071)
XLA Ops:
  8.7 0.7 convert_multiply_fusion
  9.4 41.5 %all_gather.16 = f32[2,8192]{1,0:T(2,128)S(1)} all-gather(f32[2,256]{1,0:T(2,128)S(1)} %convert_multiply_fusion), channel_id=1, replica_groups=mesh['row'=8,'col'=32] {'col'}, dimensions={1}, use_global_device_ids=true | all-gather | bytes 67584 | tf_op jit(solution)/shard_map/all_gather | solution.py:26
  50.9 39.2 %all-gather.1 = f32[32,2,256]{2,1,0:T(2,128)S(1)} all-gather(f32[1,2,256]{2,1,0:T(2,128)} %bitcast.23), channel_id=2, replica_groups=mesh['row'=8,'col'=32] {'col'}, dimensions={0}, use_global_device_ids=true | all-gather | bytes 67584 | tf_op jit(solution)/shard_map/all_gather | solution.py:25
  90.8 23.1 %all-gather.5.cloned.1.call-done = f32[256,8192]{1,0:T(8,128)} async-done(((f32[256,256]{1,0:T(8,128)}), f32[256,8192]{1,0:T(8,128)}) %all-gather.5.cloned.1.call-update) | async-done | bytes 8388624 | tf_op jit(solution)/shard_map/all_gather | solution.py:23
  113.9 102.9 %all-gather.7.cloned.1.call-done = f32[256,8192]{1,0:T(8,128)} async-done(((f32[256,256]{1,0:T(8,128)}), f32[256,8192]{1,0:T(8,128)}) %all-gather.7.cloned.1.call-update) | async-done | bytes 8388624 | tf_op jit(solution)/shard_map/all_gather | solution.py:24
  216.8 68.3 %while.18 = (s32[]{:T(128)}, f32[256,512]{1,0:T(8,128)S(1)}, f32[256,512]{1,0:T(8,128)S(1)}, f32[512]{0:T(512)S(1)}, f32[256,8192]{1,0:T(8,128)}, /*index=5*/pre...) while((s32[]{:T(128)}, f32[256,512]{1,0:T(8,128)S(1)}, ...), condition=%wide.region_2.3_spmd.clone, body=%wide.region_0.2_spmd.clone.sunk | while | flops 3229093376 | bytes 12669679 | solution.py:47
  216.9 1.9 multiply_reduce_fusion.3
  218.8 3.3 %fusion.17 = f32[256,512]{1,0:T(8,128)S(1)} fusion(f32[2,1024,512]{2,1,0:T(8,128)S(1)} %get-tuple-element.347, f32[256,8192]{1,0:T(8,128)} %get-tuple-element.389, s32[]{:T(128)S(6)} %select_n.28, f32[256,512]{1,0:T(8,128)S(1)} %get-tuple-element.366, pred[]{:T(512)S(6)} %compare.3), kind=kOutput, calls=%fused_computation.9.clone.1 | convolution fusion | flops 1610874880 | bytes 4194309 | tf_op jit(solution)/shard_map/while/body/eval_jaxpr/dot_general | solution.py:42
  222.1 3.3 %fusion.16 = f32[256,512]{1,0:T(8,128)S(1)} fusion(f32[2,1024,512]{2,1,0:T(8,128)S(1)} %get-tuple-element.347, f32[256,8192]{1,0:T(8,128)} %get-tuple-element.383, s32[]{:T(128)S(6)} %select_n.28, f32[256,512]{1,0:T(8,128)S(1)} %get-tuple-element.365, pred[]{:T(512)S(6)} %compare.3), kind=kOutput, calls=%fused_computation.8.clone.1 | convolution fusion | flops 1610874880 | bytes 4194309 | tf_op jit(solution)/shard_map/while/body/eval_jaxpr/dot_general | solution.py:39
  225.5 1.9 multiply_reduce_fusion.3
  227.4 3.3 %fusion.17 = f32[256,512]{1,0:T(8,128)S(1)} fusion(f32[2,1024,512]{2,1,0:T(8,128)S(1)} %get-tuple-element.347, f32[256,8192]{1,0:T(8,128)} %get-tuple-element.389, s32[]{:T(128)S(6)} %select_n.28, f32[256,512]{1,0:T(8,128)S(1)} %get-tuple-element.366, pred[]{:T(512)S(6)} %compare.3), kind=kOutput, calls=%fused_computation.9.clone.1 | convolution fusion | flops 1610874880 | bytes 4194309 | tf_op jit(solution)/shard_map/while/body/eval_jaxpr/dot_general | solution.py:42
  230.6 3.3 %fusion.16 = f32[256,512]{1,0:T(8,128)S(1)} fusion(f32[2,1024,512]{2,1,0:T(8,128)S(1)} %get-tuple-element.347, f32[256,8192]{1,0:T(8,128)} %get-tuple-element.383, s32[]{:T(128)S(6)} %select_n.28, f32[256,512]{1,0:T(8,128)S(1)} %get-tuple-element.365, pred[]{:T(512)S(6)} %compare.3), kind=kOutput, calls=%fused_computation.8.clone.1 | convolution fusion | flops 1610874880 | bytes 4194309 | tf_op jit(solution)/shard_map/while/body/eval_jaxpr/dot_general | solution.py:39
  234.0 1.9 multiply_reduce_fusion.3
  235.9 3.3 %fusion.17 = f32[256,512]{1,0:T(8,128)S(1)} fusion(f32[2,1024,512]{2,1,0:T(8,128)S(1)} %get-tuple-element.347, f32[256,8192]{1,0:T(8,128)} %get-tuple-element.389, s32[]{:T(128)S(6)} %select_n.28, f32[256,512]{1,0:T(8,128)S(1)} %get-tuple-element.366, pred[]{:T(512)S(6)} %compare.3), kind=kOutput, calls=%fused_computation.9.clone.1 | convolution fusion | flops 1610874880 | bytes 4194309 | tf_op jit(solution)/shard_map/while/body/eval_jaxpr/dot_general | solution.py:42
  239.2 3.3 %fusion.16 = f32[256,512]{1,0:T(8,128)S(1)} fusion(f32[2,1024,512]{2,1,0:T(8,128)S(1)} %get-tuple-element.347, f32[256,8192]{1,0:T(8,128)} %get-tuple-element.383, s32[]{:T(128)S(6)} %select_n.28, f32[256,512]{1,0:T(8,128)S(1)} %get-tuple-element.365, pred[]{:T(512)S(6)} %compare.3), kind=kOutput, calls=%fused_computation.8.clone.1 | convolution fusion | flops 1610874880 | bytes 4194309 | tf_op jit(solution)/shard_map/while/body/eval_jaxpr/dot_general | solution.py:39
  242.6 1.9 multiply_reduce_fusion.3
  244.5 3.3 %fusion.17 = f32[256,512]{1,0:T(8,128)S(1)} fusion(f32[2,1024,512]{2,1,0:T(8,128)S(1)} %get-tuple-element.347, f32[256,8192]{1,0:T(8,128)} %get-tuple-element.389, s32[]{:T(128)S(6)} %select_n.28, f32[256,512]{1,0:T(8,128)S(1)} %get-tuple-element.366, pred[]{:T(512)S(6)} %compare.3), kind=kOutput, calls=%fused_computation.9.clone.1 | convolution fusion | flops 1610874880 | bytes 4194309 | tf_op jit(solution)/shard_map/while/body/eval_jaxpr/dot_general | solution.py:42
  247.7 3.3 %fusion.16 = f32[256,512]{1,0:T(8,128)S(1)} fusion(f32[2,1024,512]{2,1,0:T(8,128)S(1)} %get-tuple-element.347, f32[256,8192]{1,0:T(8,128)} %get-tuple-element.383, s32[]{:T(128)S(6)} %select_n.28, f32[256,512]{1,0:T(8,128)S(1)} %get-tuple-element.365, pred[]{:T(512)S(6)} %compare.3), kind=kOutput, calls=%fused_computation.8.clone.1 | convolution fusion | flops 1610874880 | bytes 4194309 | tf_op jit(solution)/shard_map/while/body/eval_jaxpr/dot_general | solution.py:39
  251.1 1.9 multiply_reduce_fusion.3
  253.0 3.3 %fusion.17 = f32[256,512]{1,0:T(8,128)S(1)} fusion(f32[2,1024,512]{2,1,0:T(8,128)S(1)} %get-tuple-element.347, f32[256,8192]{1,0:T(8,128)} %get-tuple-element.389, s32[]{:T(128)S(6)} %select_n.28, f32[256,512]{1,0:T(8,128)S(1)} %get-tuple-element.366, pred[]{:T(512)S(6)} %compare.3), kind=kOutput, calls=%fused_computation.9.clone.1 | convolution fusion | flops 1610874880 | bytes 4194309 | tf_op jit(solution)/shard_map/while/body/eval_jaxpr/dot_general | solution.py:42
  256.3 3.3 %fusion.16 = f32[256,512]{1,0:T(8,128)S(1)} fusion(f32[2,1024,512]{2,1,0:T(8,128)S(1)} %get-tuple-element.347, f32[256,8192]{1,0:T(8,128)} %get-tuple-element.383, s32[]{:T(128)S(6)} %select_n.28, f32[256,512]{1,0:T(8,128)S(1)} %get-tuple-element.365, pred[]{:T(512)S(6)} %compare.3), kind=kOutput, calls=%fused_computation.8.clone.1 | convolution fusion | flops 1610874880 | bytes 4194309 | tf_op jit(solution)/shard_map/while/body/eval_jaxpr/dot_general | solution.py:39
  259.6 1.9 multiply_reduce_fusion.3
  261.5 3.3 %fusion.17 = f32[256,512]{1,0:T(8,128)S(1)} fusion(f32[2,1024,512]{2,1,0:T(8,128)S(1)} %get-tuple-element.347, f32[256,8192]{1,0:T(8,128)} %get-tuple-element.389, s32[]{:T(128)S(6)} %select_n.28, f32[256,512]{1,0:T(8,128)S(1)} %get-tuple-element.366, pred[]{:T(512)S(6)} %compare.3), kind=kOutput, calls=%fused_computation.9.clone.1 | convolution fusion | flops 1610874880 | bytes 4194309 | tf_op jit(solution)/shard_map/while/body/eval_jaxpr/dot_general | solution.py:42
  264.8 3.3 %fusion.16 = f32[256,512]{1,0:T(8,128)S(1)} fusion(f32[2,1024,512]{2,1,0:T(8,128)S(1)} %get-tuple-element.347, f32[256,8192]{1,0:T(8,128)} %get-tuple-element.383, s32[]{:T(128)S(6)} %select_n.28, f32[256,512]{1,0:T(8,128)S(1)} %get-tuple-element.365, pred[]{:T(512)S(6)} %compare.3), kind=kOutput, calls=%fused_computation.8.clone.1 | convolution fusion | flops 1610874880 | bytes 4194309 | tf_op jit(solution)/shard_map/while/body/eval_jaxpr/dot_general | solution.py:39
  268.2 1.9 multiply_reduce_fusion.3
  270.1 3.3 %fusion.17 = f32[256,512]{1,0:T(8,128)S(1)} fusion(f32[2,1024,512]{2,1,0:T(8,128)S(1)} %get-tuple-element.347, f32[256,8192]{1,0:T(8,128)} %get-tuple-element.389, s32[]{:T(128)S(6)} %select_n.28, f32[256,512]{1,0:T(8,128)S(1)} %get-tuple-element.366, pred[]{:T(512)S(6)} %compare.3), kind=kOutput, calls=%fused_computation.9.clone.1 | convolution fusion | flops 1610874880 | bytes 4194309 | tf_op jit(solution)/shard_map/while/body/eval_jaxpr/dot_general | solution.py:42
  273.3 3.3 %fusion.16 = f32[256,512]{1,0:T(8,128)S(1)} fusion(f32[2,1024,512]{2,1,0:T(8,128)S(1)} %get-tuple-element.347, f32[256,8192]{1,0:T(8,128)} %get-tuple-element.383, s32[]{:T(128)S(6)} %select_n.28, f32[256,512]{1,0:T(8,128)S(1)} %get-tuple-element.365, pred[]{:T(512)S(6)} %compare.3), kind=kOutput, calls=%fused_computation.8.clone.1 | convolution fusion | flops 1610874880 | bytes 4194309 | tf_op jit(solution)/shard_map/while/body/eval_jaxpr/dot_general | solution.py:39
  276.7 1.9 multiply_reduce_fusion.3
  278.6 3.3 %fusion.17 = f32[256,512]{1,0:T(8,128)S(1)} fusion(f32[2,1024,512]{2,1,0:T(8,128)S(1)} %get-tuple-element.347, f32[256,8192]{1,0:T(8,128)} %get-tuple-element.389, s32[]{:T(128)S(6)} %select_n.28, f32[256,512]{1,0:T(8,128)S(1)} %get-tuple-element.366, pred[]{:T(512)S(6)} %compare.3), kind=kOutput, calls=%fused_computation.9.clone.1 | convolution fusion | flops 1610874880 | bytes 4194309 | tf_op jit(solution)/shard_map/while/body/eval_jaxpr/dot_general | solution.py:42
  281.9 3.3 %fusion.16 = f32[256,512]{1,0:T(8,128)S(1)} fusion(f32[2,1024,512]{2,1,0:T(8,128)S(1)} %get-tuple-element.347, f32[256,8192]{1,0:T(8,128)} %get-tuple-element.383, s32[]{:T(128)S(6)} %select_n.28, f32[256,512]{1,0:T(8,128)S(1)} %get-tuple-element.365, pred[]{:T(512)S(6)} %compare.3), kind=kOutput, calls=%fused_computation.8.clone.1 | convolution fusion | flops 1610874880 | bytes 4194309 | tf_op jit(solution)/shard_map/while/body/eval_jaxpr/dot_general | solution.py:39
  286.0 1.1 multiply_reduce_fusion.1
  287.1 15.6 %psum.7 = f32[512]{0:T(512)S(1)} all-reduce(f32[512]{0:T(512)S(1)} %get-tuple-element.266), channel_id=1, replica_groups=mesh['row'=8,'col'=32] {'row'}, use_global_device_ids=true, to_apply=%region_4.5 | all-reduce | flops 512 | bytes 4096 | tf_op jit(solution)/shard_map/psum | solution.py:56
  (51 shorter events, 4.3 us)
Async XLA Ops:
  7.2 106.8 %all-gather.5.cloned.1.call-start = ((), (), s32[]{:S(2)}) async-start(), calls=%async_computation | async-start | bytes 8650752 | tf_op jit(solution)/shard_map/all_gather | solution.py:23
  7.9 209.0 %all-gather.7.cloned.1.call-start = ((), (), s32[]{:S(2)}) async-start(), calls=%async_computation.1 | async-start | bytes 8650752 | tf_op jit(solution)/shard_map/all_gather | solution.py:24
Sparse Core Ops, SparseCore 0:
  10.4 103.4 all-gather.4
  116.4 100.4 all-gather.6
